TPU v7x, 32 devices: a whole 2x2x4 slice. The times are simulated.
32 devices in a mesh: dp: 8 (over z, x), table: 4 (over y, core).
Axes of the slice: x: 2, y: 2, z: 4, core: 2. Of those that a mesh axis runs over, the one named last changes fastest.
Arguments:
- feature_high: int32 [20, 2048], P(None, 'dp'), may hold values from 0 to 2047
- feature_low: int32 [20, 2048], P(None, 'dp'), may hold values from 0 to 2047
- labels: int32 [2048], P('dp'), may hold values 0 or 1
- weights: float32 [4194304], P(('dp', 'table')), may hold values from -0.6 to 0.6
- history_steps: float32 [8, 4194304], P(None, ('dp', 'table')), may hold values from -46 to 46
- history_diffs: float32 [8, 4194304], P(None, ('dp', 'table')), may hold values from -198 to 198, as said below
Outputs:
- direction: float32 [4194304], P(('dp', 'table'))
Inputs may be any that keep to these rules, and one draw needn't show every extreme that they name: Each entry of history_diffs has the sign of the matching entry of history_steps and 0.2 to 4.3 times its magnitude.
All inputs are finite; a program needn't handle non-finite values. No bound on the sum of `labels` on one device may be relied on, other than what follows from the above.
Results may differ from a plain program's by a relative error of at most 0.0001.
Values sent between devices are 32-bit elements; how exact they have to be, the bound alone decides.
A program may use at most 64 MiB of HBM per device.

v0:
```python
import jax
import jax.numpy as jnp
from jax import lax
from jax.sharding import PartitionSpec as P

TABLE = 4194304
HASHES = 4
high_mult = (40503, 96469, 255361, 362443)
low_mult = (2053, 6151, 12289, 98317)
slot_mult = (1543, 3079, 769, 3457)
shifts = (0, 1048573, 2097143, 3145727)
l2_weight = 1.0


def hashed(feature_high, feature_low, number):
    slot_index = jnp.arange(feature_high.shape[0], dtype=jnp.int32)[:, None]
    part_high = feature_high * high_mult[number] % TABLE
    part_low = feature_low * low_mult[number] % TABLE
    return (part_high + part_low + slot_index * slot_mult[number] + shifts[number]) % TABLE


def local(feature_high, feature_low, labels, weights, history_steps, history_diffs):
    width = weights.shape[0]
    shard_count = lax.axis_size("table")
    column = lax.axis_index("table")
    gathered = lax.all_gather(weights, "dp", axis=0, tiled=True)
    margin = jnp.zeros((feature_high.shape[1],), jnp.float32)
    owned_list = []
    position_list = []
    for number in range(HASHES):
        indices = hashed(feature_high, feature_low, number)
        blocks = indices // width
        owned = blocks % shard_count == column
        position = blocks // shard_count * width + indices % width
        owned_list.append(owned)
        position_list.append(position)
        margin = margin + jnp.sum(jnp.where(owned, gathered[position], 0.0), axis=0)
    margin = lax.psum(margin, "table")
    residual = jax.nn.sigmoid(margin) - labels.astype(jnp.float32)
    all_positions = jnp.concatenate([place.reshape(-1) for place in position_list])
    all_terms = jnp.concatenate(
        [jnp.where(owned, residual[None, :], 0.0).reshape(-1) for owned in owned_list]
    )
    partial_grad = jnp.zeros(gathered.shape, jnp.float32).at[all_positions].add(all_terms)
    summed = lax.psum(partial_grad, "dp")
    mine = lax.dynamic_slice_in_dim(summed, lax.axis_index("dp") * width, width)
    gradient = mine + l2_weight * weights
    memory = history_steps.shape[0]
    newest = memory - 1
    pair_sums, newest_square = lax.psum(
        (
            jnp.sum(history_steps * history_diffs, axis=1),
            jnp.sum(history_diffs[newest] * history_diffs[newest]),
        ),
        ("dp", "table"),
    )
    inverse = 1.0 / pair_sums
    current = gradient
    alphas = [None] * memory
    for which in reversed(range(memory)):
        alphas[which] = inverse[which] * lax.psum(
            jnp.sum(history_steps[which] * current), ("dp", "table")
        )
        current = current - alphas[which] * history_diffs[which]
    current = pair_sums[newest] / newest_square * current
    for which in range(memory):
        correction = inverse[which] * lax.psum(
            jnp.sum(history_diffs[which] * current), ("dp", "table")
        )
        current = current + (alphas[which] - correction) * history_steps[which]
    return -current


def solution(mesh):
    placed = (
        P(None, "dp"),
        P(None, "dp"),
        P("dp"),
        P(("dp", "table")),
        P(None, ("dp", "table")),
        P(None, ("dp", "table")),
    )
    return jax.shard_map(
        local, mesh=mesh, in_specs=placed, out_specs=P(("dp", "table")), check_vma=False
    )
```

profile of v0, /device:TPU:0, one launch (start us, length us, event | category | flops | bytes accessed | tf_op | source)
XLA Modules:
  0.0 1326.4 jit_solution(4070910795745092147)
XLA Ops:
  8.8 76.8 %all-gather.2.cloned.1.call-done = f32[1048576]{0:T(1024)} async-done(((f32[131072]{0:T(1024)}), f32[1048576]{0:T(1024)}) %all-gather.2.cloned.1.call-update) | async-done | bytes 4194320 | tf_op jit(solution)/shard_map/all_gather | solution.py:26
  85.6 60.4 %gather_fusion.3 = f32[5120]{0:T(1024)S(1)} fusion(f32[1048576]{0:T(1024)} %all-gather.2.cloned.1.call-done, s32[5120]{0:T(1024)S(1)} %broadcast_clamp_fusion), kind=kCustom, calls=%fused_computation.3 | custom fusion | bytes 61440 | tf_op jit(solution)/shard_map/gather | solution.py:37
  146.0 60.4 %gather_fusion.1 = f32[5120]{0:T(1024)S(1)} fusion(f32[1048576]{0:T(1024)} %all-gather.2.cloned.1.call-done, s32[5120]{0:T(1024)S(1)} %broadcast_clamp_fusion.2), kind=kCustom, calls=%fused_computation.1 | custom fusion | bytes 61440 | tf_op jit(solution)/shard_map/gather | solution.py:37
  206.5 60.4 %gather_fusion = f32[5120]{0:T(1024)S(1)} fusion(f32[1048576]{0:T(1024)} %all-gather.2.cloned.1.call-done, s32[5120]{0:T(1024)S(1)} %broadcast_clamp_fusion.3), kind=kCustom, calls=%fused_computation | custom fusion | bytes 61440 | tf_op jit(solution)/shard_map/gather | solution.py:37
  266.9 60.4 %gather_fusion.2 = f32[5120]{0:T(1024)S(1)} fusion(f32[1048576]{0:T(1024)} %all-gather.2.cloned.1.call-done, s32[5120]{0:T(1024)S(1)} %broadcast_clamp_fusion.1), kind=kCustom, calls=%fused_computation.2 | custom fusion | bytes 61440 | tf_op jit(solution)/shard_map/gather | solution.py:37
  333.3 109.3 %scatter_custom_fusion = f32[1048576]{0:T(1024)} fusion(s32[20480]{0:T(1024)S(1)} %bitcast.84, f32[20480]{0:T(1024)S(1)} %pad_maximum_fusion, f32[]{:T(128)} %constant.207.clone.1), kind=kCustom, calls=%fused_computation.6 | custom fusion | flops 20480 | bytes 4194308 | tf_op jit(solution)/shard_map/scatter-add | solution.py:44
  463.9 133.7 %all-reduce.4.cloned.1.call-done = f32[1048576]{0:T(1024)} async-done(((f32[1048576]{0:T(1024)}), f32[1048576]{0:T(1024)}) %all-reduce.4.cloned.1.call-update) | async-done | bytes 4194320 | tf_op jit(solution)/shard_map/psum | solution.py:45
  599.4 16.6 %fusion.61 = (f32[1,131072]{1,0:T(1,128)}, f32[1,131072]{1,0:T(1,128)S(1)}, f32[1,131072]{1,0:T(1,128)}, f32[1,131072]{1,0:T(1,128)S(1)}, f32[1,131072]{1,0:T(1,...) fusion(f32[8,131072]{1,0:T(8,128)} %param.11), kind=kLoop, calls=%fused_computation.206 | loop fusion | bytes 8388608 | tf_op jit(solution)/shard_map/slice | solution.py:64
  616.0 39.4 %all-reduce.1 = (f32[8]{0:T(128)S(1)}, f32[]{:T(128)}) all-reduce(f32[8]{0:T(128)S(1)} %multiply_reduce_fusion, f32[]{:T(128)} %multiply_reduce_fusion.16), channel_id=1, replica_groups=mesh['dp'=8,'table'=4] {'dp','table'}, use_global_device_ids=true, to_apply=%region_1.2 | all-reduce | flops 9 | bytes 72 | tf_op jit(solution)/shard_map/psum | solution.py:50
  660.4 40.3 %psum.145 = f32[]{:T(128)} all-reduce(f32[]{:T(128)} %get-tuple-element.23), channel_id=1, replica_groups=mesh['dp'=8,'table'=4] {'dp','table'}, use_global_device_ids=true, to_apply=%region_14.15 | all-reduce | flops 1 | bytes 8 | tf_op jit(solution)/shard_map/psum | solution.py:61
  703.8 40.7 %psum.146 = f32[]{:T(128)} all-reduce(f32[]{:T(128)} %multiply_reduce_fusion.14), channel_id=1, replica_groups=mesh['dp'=8,'table'=4] {'dp','table'}, use_global_device_ids=true, to_apply=%region_16.17 | all-reduce | flops 1 | bytes 8 | tf_op jit(solution)/shard_map/psum | solution.py:61
  748.7 40.4 %psum.147 = f32[]{:T(128)} all-reduce(f32[]{:T(128)} %get-tuple-element.21), channel_id=1, replica_groups=mesh['dp'=8,'table'=4] {'dp','table'}, use_global_device_ids=true, to_apply=%region_18.19 | all-reduce | flops 1 | bytes 8 | tf_op jit(solution)/shard_map/psum | solution.py:61
  792.3 40.6 %psum.148 = f32[]{:T(128)} all-reduce(f32[]{:T(128)} %multiply_reduce_fusion.12), channel_id=1, replica_groups=mesh['dp'=8,'table'=4] {'dp','table'}, use_global_device_ids=true, to_apply=%region_20.21 | all-reduce | flops 1 | bytes 8 | tf_op jit(solution)/shard_map/psum | solution.py:61
  837.1 40.3 %psum.149 = f32[]{:T(128)} all-reduce(f32[]{:T(128)} %get-tuple-element.19), channel_id=1, replica_groups=mesh['dp'=8,'table'=4] {'dp','table'}, use_global_device_ids=true, to_apply=%region_22.23 | all-reduce | flops 1 | bytes 8 | tf_op jit(solution)/shard_map/psum | solution.py:61
  881.2 40.6 %psum.150 = f32[]{:T(128)} all-reduce(f32[]{:T(128)} %multiply_reduce_fusion.10), channel_id=1, replica_groups=mesh['dp'=8,'table'=4] {'dp','table'}, use_global_device_ids=true, to_apply=%region_24.25 | all-reduce | flops 1 | bytes 8 | tf_op jit(solution)/shard_map/psum | solution.py:61
  926.0 40.2 %all-reduce = (f32[]{:T(128)}, f32[]{:T(128)}) all-reduce(f32[]{:T(128)} %get-tuple-element.17, f32[]{:T(128)} %get-tuple-element.61), channel_id=1, replica_groups=mesh['dp'=8,'table'=4] {'dp','table'}, use_global_device_ids=true, to_apply=%region_26.27 | all-reduce | flops 2 | bytes 16 | tf_op jit(solution)/shard_map/psum | solution.py:61
  970.7 40.6 %psum.152 = f32[]{:T(128)} all-reduce(f32[]{:T(128)} %multiply_reduce_fusion.8), channel_id=1, replica_groups=mesh['dp'=8,'table'=4] {'dp','table'}, use_global_device_ids=true, to_apply=%region_28.29 | all-reduce | flops 1 | bytes 8 | tf_op jit(solution)/shard_map/psum | solution.py:67
  1015.6 40.1 %psum.153 = f32[]{:T(128)} all-reduce(f32[]{:T(128)} %get-tuple-element.15), channel_id=1, replica_groups=mesh['dp'=8,'table'=4] {'dp','table'}, use_global_device_ids=true, to_apply=%region_30.31 | all-reduce | flops 1 | bytes 8 | tf_op jit(solution)/shard_map/psum | solution.py:67
  1058.8 40.7 %psum.154 = f32[]{:T(128)} all-reduce(f32[]{:T(128)} %multiply_reduce_fusion.6), channel_id=1, replica_groups=mesh['dp'=8,'table'=4] {'dp','table'}, use_global_device_ids=true, to_apply=%region_32.33 | all-reduce | flops 1 | bytes 8 | tf_op jit(solution)/shard_map/psum | solution.py:67
  1103.7 40.1 %psum.155 = f32[]{:T(128)} all-reduce(f32[]{:T(128)} %get-tuple-element.13), channel_id=1, replica_groups=mesh['dp'=8,'table'=4] {'dp','table'}, use_global_device_ids=true, to_apply=%region_34.35 | all-reduce | flops 1 | bytes 8 | tf_op jit(solution)/shard_map/psum | solution.py:67
  1147.2 40.7 %psum.156 = f32[]{:T(128)} all-reduce(f32[]{:T(128)} %multiply_reduce_fusion.4), channel_id=1, replica_groups=mesh['dp'=8,'table'=4] {'dp','table'}, use_global_device_ids=true, to_apply=%region_36.37 | all-reduce | flops 1 | bytes 8 | tf_op jit(solution)/shard_map/psum | solution.py:67
  1191.4 40.2 %psum.157 = f32[]{:T(128)} all-reduce(f32[]{:T(128)} %get-tuple-element.11), channel_id=1, replica_groups=mesh['dp'=8,'table'=4] {'dp','table'}, use_global_device_ids=true, to_apply=%region_38.39 | all-reduce | flops 1 | bytes 8 | tf_op jit(solution)/shard_map/psum | solution.py:67
  1233.7 40.6 %psum.158 = f32[]{:T(128)} all-reduce(f32[]{:T(128)} %multiply_reduce_fusion.2), channel_id=1, replica_groups=mesh['dp'=8,'table'=4] {'dp','table'}, use_global_device_ids=true, to_apply=%region_40.41 | all-reduce | flops 1 | bytes 8 | tf_op jit(solution)/shard_map/psum | solution.py:67
  1277.3 40.1 %psum.159 = f32[]{:T(128)} all-reduce(f32[]{:T(128)} %get-tuple-element.9), channel_id=1, replica_groups=mesh['dp'=8,'table'=4] {'dp','table'}, use_global_device_ids=true, to_apply=%region_42.43 | all-reduce | flops 1 | bytes 8 | tf_op jit(solution)/shard_map/psum | solution.py:67
  (73 shorter events, 67.1 us)
Async XLA Ops:
  6.5 79.1 %all-gather.2.cloned.1.call-start = ((), (), s32[]{:S(2)}) async-start(), calls=%async_computation | async-start | bytes 4718592 | tf_op jit(solution)/shard_map/all_gather | solution.py:26
  7.3 590.4 %all-reduce.4.cloned.1.call-start = ((), (), s32[]{:S(2)}) async-start(), calls=%async_computation.1 | async-start | bytes 8388608 | tf_op jit(solution)/shard_map/psum | solution.py:45
  266.9 66.3 %copy-start.4 = (s32[256]{0:T(256)S(1)}, s32[256]{0:T(256)}, u32[]{:S(2)}) copy-start(s32[256]{0:T(256)} %param.8) | copy-start | bytes 3076
  459.1 138.6 %copy-start = (f32[1,131072]{1,0:T(1,128)}, f32[1,131072]{1,0:T(1,128)S(1)}, u32[]{:S(2)}) copy-start(f32[1,131072]{1,0:T(1,128)S(1)} %get-tuple-element.59) | copy-start | bytes 1572868
  459.1 138.6 %copy-start.3 = (f32[131072]{0:T(1024)S(1)}, f32[131072]{0:T(1024)}, u32[]{:S(2)}) copy-start(f32[131072]{0:T(1024)} %param.9) | copy-start | bytes 1572868
  1100.8 174.7 %copy-start.2 = (f32[1,131072]{1,0:T(1,128)S(1)}, f32[1,131072]{1,0:T(1,128)}, u32[]{:S(2)}) copy-start(f32[1,131072]{1,0:T(1,128)} %get-tuple-element.58) | copy-start | bytes 1572868
  1145.3 173.4 %copy-start.1 = (f32[1,131072]{1,0:T(1,128)S(1)}, f32[1,131072]{1,0:T(1,128)}, u32[]{:S(2)}) copy-start(f32[1,131072]{1,0:T(1,128)} %copy-done) | copy-start | bytes 1572868
Sparse Core Ops, SparseCore 0:
  9.5 76.0 all-gather.1
  442.8 154.8 all-reduce.3
where the time goes:
time: 1340 us; the launch traced here: 1330 us
  blocking collectives  651 us (49%)
  local copies, waits for them, and re-layouts  276 us (21%)
  waiting for transfers between devices  211 us (16%)
  other arithmetic  152 us (11%)
  between operations  35.7 us (3%)
    psum x8, blocking collectives, local(): lax.psum(jnp.sum(history_diffs[which] * current), ('dp', 'table'))  323 us
    psum x7, blocking collectives, local(): lax.psum(jnp.sum(history_steps[which] * current), ('dp', 'table'))  283 us
    gather x8, local copies, waits for them, and re-layouts, local(): margin = margin + jnp.sum(jnp.where(owned, gathered[position], 0.0), axis=0)  242 us
    psum x1, waiting for transfers between devices, local(): summed = lax.psum(partial_grad, 'dp')  134 us
    scatter-add x1, other arithmetic, local(): jnp.zeros(gathered.shape, jnp.float32).at[all_positions].add(all_terms)  109 us
    all_gather x1, waiting for transfers between devices, local(): gathered = lax.all_gather(weights, 'dp', axis=0, tiled=True)  76.8 us
    psum x1, blocking collectives, local(): lax.psum((jnp.sum(history_steps * history_diffs, axis=1), jnp.sum(history...  39.4 us
  transfers between devices with their start and end apart: 2, of which 2 were waited for; matrix products, arithmetic and copies ran while one was open for 2% of the time, Pallas kernels for 0%

commit v1 on v0

--- a/solution.py
+++ b/solution.py
@@ -48,11 +48,14 @@
     memory = history_steps.shape[0]
     newest = memory - 1
     pair_sums, newest_square = lax.psum(
-        (
-            jnp.sum(history_steps * history_diffs, axis=1),
-            jnp.sum(history_diffs[newest] * history_diffs[newest]),
+        lax.psum(
+            (
+                jnp.sum(history_steps * history_diffs, axis=1),
+                jnp.sum(history_diffs[newest] * history_diffs[newest]),
+            ),
+            "table",
         ),
-        ("dp", "table"),
+        "dp",
     )
     inverse = 1.0 / pair_sums
     current = gradient

time: 1340 us -> 1320 us (0.985)
  waiting for transfers between devices: 211 us -> 174 us
  blocking collectives: 651 us -> 674 us
    psum x7 -> x8, blocking collectives: 283 us -> 323 us  [local(): lax.psum(jnp.sum(history_steps[which] * current), ('dp', 'table'))]
    psum x1, blocking collectives: 39.4 us -> 6.17 us  [local(): lax.psum((jnp.sum(history_steps * history_diffs, axis=1), jnp.sum(history...]
    all_gather x1, waiting for transfers between devices: 76.8 us -> 55.7 us  [local(): gathered = lax.all_gather(weights, 'dp', axis=0, tiled=True)]
    psum x1, waiting for transfers between devices: 134 us -> 117 us  [local(): summed = lax.psum(partial_grad, 'dp')]
    psum x1, blocking collectives: 5.67 us -> 21.6 us  [local(): lax.psum(lax.psum((jnp.sum(history_steps * history_diffs, axis=1), jnp.su...]
  transfers between devices with their start and end apart: 2 -> 2, of which waited for: 2 -> 2; matrix products, arithmetic and copies ran while one was open for 2% -> 3% of each run, Pallas kernels for 0% -> 0%
where the time goes in v1:
time: 1320 us; the launch traced here: 1310 us
  blocking collectives  674 us (51%)
  local copies, waits for them, and re-layouts  276 us (21%)
  waiting for transfers between devices  174 us (13%)
  other arithmetic  152 us (12%)
  between operations  35.4 us (3%)
    psum x8, blocking collectives, local(): lax.psum(jnp.sum(history_diffs[which] * current), ('dp', 'table'))  323 us
    psum x8, blocking collectives, local(): lax.psum(jnp.sum(history_steps[which] * current), ('dp', 'table'))  323 us
    gather x8, local copies, waits for them, and re-layouts, local(): margin = margin + jnp.sum(jnp.where(owned, gathered[position], 0.0), axis=0)  242 us
    psum x1, waiting for transfers between devices, local(): summed = lax.psum(partial_grad, 'dp')  117 us
    scatter-add x1, other arithmetic, local(): jnp.zeros(gathered.shape, jnp.float32).at[all_positions].add(all_terms)  109 us
    all_gather x1, waiting for transfers between devices, local(): gathered = lax.all_gather(weights, 'dp', axis=0, tiled=True)  55.7 us
  transfers between devices with their start and end apart: 2, of which 2 were waited for; matrix products, arithmetic and copies ran while one was open for 3% of the time, Pallas kernels for 0%

profile of v1, /device:TPU:0, one launch (start us, length us, event | category | flops | bytes accessed | tf_op | source)
XLA Modules:
  0.0 1311.4 jit_solution(15483540241528861007)
XLA Ops:
  30.0 55.7 %all-gather.2.cloned.1.call-done = f32[1048576]{0:T(1024)} async-done(((f32[131072]{0:T(1024)}), f32[1048576]{0:T(1024)}) %all-gather.2.cloned.1.call-update) | async-done | bytes 4194320 | tf_op jit(solution)/shard_map/all_gather | solution.py:26
  85.6 60.4 %gather_fusion = f32[5120]{0:T(1024)S(1)} fusion(f32[1048576]{0:T(1024)} %all-gather.2.cloned.1.call-done, s32[5120]{0:T(1024)S(1)} %broadcast_clamp_fusion.3), kind=kCustom, calls=%fused_computation | custom fusion | bytes 61440 | tf_op jit(solution)/shard_map/gather | solution.py:37
  146.0 60.4 %gather_fusion.1 = f32[5120]{0:T(1024)S(1)} fusion(f32[1048576]{0:T(1024)} %all-gather.2.cloned.1.call-done, s32[5120]{0:T(1024)S(1)} %broadcast_clamp_fusion.2), kind=kCustom, calls=%fused_computation.1 | custom fusion | bytes 61440 | tf_op jit(solution)/shard_map/gather | solution.py:37
  206.5 60.4 %gather_fusion.2 = f32[5120]{0:T(1024)S(1)} fusion(f32[1048576]{0:T(1024)} %all-gather.2.cloned.1.call-done, s32[5120]{0:T(1024)S(1)} %broadcast_clamp_fusion.1), kind=kCustom, calls=%fused_computation.2 | custom fusion | bytes 61440 | tf_op jit(solution)/shard_map/gather | solution.py:37
  266.9 60.4 %gather_fusion.3 = f32[5120]{0:T(1024)S(1)} fusion(f32[1048576]{0:T(1024)} %all-gather.2.cloned.1.call-done, s32[5120]{0:T(1024)S(1)} %broadcast_clamp_fusion), kind=kCustom, calls=%fused_computation.3 | custom fusion | bytes 61440 | tf_op jit(solution)/shard_map/gather | solution.py:37
  333.9 109.3 %scatter_custom_fusion = f32[1048576]{0:T(1024)} fusion(s32[20480]{0:T(1024)S(1)} %bitcast.85, f32[20480]{0:T(1024)S(1)} %pad_maximum_fusion, f32[]{:T(128)} %constant.207.clone.1), kind=kCustom, calls=%fused_computation.6 | custom fusion | flops 20480 | bytes 4194308 | tf_op jit(solution)/shard_map/scatter-add | solution.py:44
  459.7 21.6 %all-reduce = (f32[8]{0:T(128)S(1)}, f32[]{:T(128)}) all-reduce(f32[8]{0:T(128)S(1)} %get-tuple-element.7, f32[]{:T(128)} %get-tuple-element.8), channel_id=1, replica_groups=mesh['dp'=8,'table'=4] {'dp'}, use_global_device_ids=true, to_apply=%region_2.3 | all-reduce | flops 9 | bytes 72 | tf_op jit(solution)/shard_map/psum | solution.py:50
  481.4 117.2 %all-reduce.4.cloned.1.call-done = f32[1048576]{0:T(1024)} async-done(((f32[1048576]{0:T(1024)}), f32[1048576]{0:T(1024)}) %all-reduce.4.cloned.1.call-update) | async-done | bytes 4194320 | tf_op jit(solution)/shard_map/psum | solution.py:45
  601.3 39.4 %psum.160 = f32[]{:T(128)} all-reduce(f32[]{:T(128)} %multiply_reduce_fusion.16), channel_id=1, replica_groups=mesh['dp'=8,'table'=4] {'dp','table'}, use_global_device_ids=true, to_apply=%region_14.15 | all-reduce | flops 1 | bytes 8 | tf_op jit(solution)/shard_map/psum | solution.py:64
  644.8 40.4 %psum.161 = f32[]{:T(128)} all-reduce(f32[]{:T(128)} %get-tuple-element.24), channel_id=1, replica_groups=mesh['dp'=8,'table'=4] {'dp','table'}, use_global_device_ids=true, to_apply=%region_16.17 | all-reduce | flops 1 | bytes 8 | tf_op jit(solution)/shard_map/psum | solution.py:64
  688.4 40.7 %psum.162 = f32[]{:T(128)} all-reduce(f32[]{:T(128)} %multiply_reduce_fusion.14), channel_id=1, replica_groups=mesh['dp'=8,'table'=4] {'dp','table'}, use_global_device_ids=true, to_apply=%region_18.19 | all-reduce | flops 1 | bytes 8 | tf_op jit(solution)/shard_map/psum | solution.py:64
  733.4 40.4 %psum.163 = f32[]{:T(128)} all-reduce(f32[]{:T(128)} %get-tuple-element.22), channel_id=1, replica_groups=mesh['dp'=8,'table'=4] {'dp','table'}, use_global_device_ids=true, to_apply=%region_20.21 | all-reduce | flops 1 | bytes 8 | tf_op jit(solution)/shard_map/psum | solution.py:64
  777.4 40.5 %psum.164 = f32[]{:T(128)} all-reduce(f32[]{:T(128)} %multiply_reduce_fusion.12), channel_id=1, replica_groups=mesh['dp'=8,'table'=4] {'dp','table'}, use_global_device_ids=true, to_apply=%region_22.23 | all-reduce | flops 1 | bytes 8 | tf_op jit(solution)/shard_map/psum | solution.py:64
  822.2 40.4 %psum.165 = f32[]{:T(128)} all-reduce(f32[]{:T(128)} %get-tuple-element.20), channel_id=1, replica_groups=mesh['dp'=8,'table'=4] {'dp','table'}, use_global_device_ids=true, to_apply=%region_24.25 | all-reduce | flops 1 | bytes 8 | tf_op jit(solution)/shard_map/psum | solution.py:64
  867.1 40.6 %psum.166 = f32[]{:T(128)} all-reduce(f32[]{:T(128)} %multiply_reduce_fusion.10), channel_id=1, replica_groups=mesh['dp'=8,'table'=4] {'dp','table'}, use_global_device_ids=true, to_apply=%region_26.27 | all-reduce | flops 1 | bytes 8 | tf_op jit(solution)/shard_map/psum | solution.py:64
  912.0 40.3 %psum.167 = f32[]{:T(128)} all-reduce(f32[]{:T(128)} %get-tuple-element.18), channel_id=1, replica_groups=mesh['dp'=8,'table'=4] {'dp','table'}, use_global_device_ids=true, to_apply=%region_28.29 | all-reduce | flops 1 | bytes 8 | tf_op jit(solution)/shard_map/psum | solution.py:64
  955.6 40.7 %psum.168 = f32[]{:T(128)} all-reduce(f32[]{:T(128)} %multiply_reduce_fusion.8), channel_id=1, replica_groups=mesh['dp'=8,'table'=4] {'dp','table'}, use_global_device_ids=true, to_apply=%region_30.31 | all-reduce | flops 1 | bytes 8 | tf_op jit(solution)/shard_map/psum | solution.py:70
  1000.7 40.3 %psum.169 = f32[]{:T(128)} all-reduce(f32[]{:T(128)} %get-tuple-element.16), channel_id=1, replica_groups=mesh['dp'=8,'table'=4] {'dp','table'}, use_global_device_ids=true, to_apply=%region_32.33 | all-reduce | flops 1 | bytes 8 | tf_op jit(solution)/shard_map/psum | solution.py:70
  1044.3 40.6 %psum.170 = f32[]{:T(128)} all-reduce(f32[]{:T(128)} %multiply_reduce_fusion.6), channel_id=1, replica_groups=mesh['dp'=8,'table'=4] {'dp','table'}, use_global_device_ids=true, to_apply=%region_34.35 | all-reduce | flops 1 | bytes 8 | tf_op jit(solution)/shard_map/psum | solution.py:70
  1089.1 40.2 %psum.171 = f32[]{:T(128)} all-reduce(f32[]{:T(128)} %get-tuple-element.14), channel_id=1, replica_groups=mesh['dp'=8,'table'=4] {'dp','table'}, use_global_device_ids=true, to_apply=%region_36.37 | all-reduce | flops 1 | bytes 8 | tf_op jit(solution)/shard_map/psum | solution.py:70
  1132.5 40.6 %psum.172 = f32[]{:T(128)} all-reduce(f32[]{:T(128)} %multiply_reduce_fusion.4), channel_id=1, replica_groups=mesh['dp'=8,'table'=4] {'dp','table'}, use_global_device_ids=true, to_apply=%region_38.39 | all-reduce | flops 1 | bytes 8 | tf_op jit(solution)/shard_map/psum | solution.py:70
  1176.4 40.2 %psum.173 = f32[]{:T(128)} all-reduce(f32[]{:T(128)} %get-tuple-element.12), channel_id=1, replica_groups=mesh['dp'=8,'table'=4] {'dp','table'}, use_global_device_ids=true, to_apply=%region_40.41 | all-reduce | flops 1 | bytes 8 | tf_op jit(solution)/shard_map/psum | solution.py:70
  1218.6 40.5 %psum.174 = f32[]{:T(128)} all-reduce(f32[]{:T(128)} %multiply_reduce_fusion.2), channel_id=1, replica_groups=mesh['dp'=8,'table'=4] {'dp','table'}, use_global_device_ids=true, to_apply=%region_42.43 | all-reduce | flops 1 | bytes 8 | tf_op jit(solution)/shard_map/psum | solution.py:70
  1262.3 40.2 %psum.175 = f32[]{:T(128)} all-reduce(f32[]{:T(128)} %get-tuple-element.10), channel_id=1, replica_groups=mesh['dp'=8,'table'=4] {'dp','table'}, use_global_device_ids=true, to_apply=%region_44.45 | all-reduce | flops 1 | bytes 8 | tf_op jit(solution)/shard_map/psum | solution.py:70
  (73 shorter events, 84.6 us)
Async XLA Ops:
  6.5 79.1 %all-gather.2.cloned.1.call-start = ((), (), s32[]{:S(2)}) async-start(), calls=%async_computation | async-start | bytes 4718592 | tf_op jit(solution)/shard_map/all_gather | solution.py:26
  7.3 16.7 %copy-start.1 = (s32[20,256]{1,0:T(8,128)S(1)}, s32[20,256]{1,0:T(8,128)}, u32[]{:S(2)}) copy-start(s32[20,256]{1,0:T(8,128)} %param.7) | copy-start | bytes 61444
  7.3 16.7 %copy-start.2 = (s32[20,256]{1,0:T(8,128)S(1)}, s32[20,256]{1,0:T(8,128)}, u32[]{:S(2)}) copy-start(s32[20,256]{1,0:T(8,128)} %param.6) | copy-start | bytes 61444
  7.3 591.3 %all-reduce.4.cloned.1.call-start = ((), (), s32[]{:S(2)}) async-start(), calls=%async_computation.1 | async-start | bytes 8388608 | tf_op jit(solution)/shard_map/psum | solution.py:45
  266.9 66.9 %copy-start.3 = (s32[256]{0:T(256)S(1)}, s32[256]{0:T(256)}, u32[]{:S(2)}) copy-start(s32[256]{0:T(256)} %param.8) | copy-start | bytes 3076
  1130.6 173.1 %copy-start = (f32[1,131072]{1,0:T(1,128)S(1)}, f32[1,131072]{1,0:T(1,128)}, u32[]{:S(2)}) copy-start(f32[1,131072]{1,0:T(1,128)} %get-tuple-element.60) | copy-start | bytes 1572868
Sparse Core Ops, SparseCore 0:
  9.5 76.0 all-gather.1
  443.4 155.1 all-reduce.3
